TPU v7x, 32 devices: a whole 2x2x4 slice. The times are simulated.
32 devices in a mesh: dp: 8 (over z, y), head: 4 (over x, core).
Axes of the slice: x: 2, y: 2, z: 4, core: 2. Of those that a mesh axis runs over, the one named last changes fastest.
Arguments:
- tokens: bfloat16 [24576, 768], P(('dp', 'head')), may hold values from -15 to 15
- segment_ids: int32 [24576], P('dp'), may hold values from 0 to 189, as said below
- cotangent: bfloat16 [24576, 768], P(('dp', 'head')), may hold values from -6 to 6
- clip_norm: float32 [1], replicated, as said below
- master_qkv: float32 [768, 2304], P('dp'), may hold values from -0.21875 to 0.21875
- master_out: float32 [768, 768], P('dp'), may hold values from -0.875 to 0.875
- master_gu: float32 [768, 6144], P('dp'), may hold values from -0.72168784 to 0.72168784
- master_down: float32 [3072, 768], P('dp'), may hold values from -0.109375 to 0.109375
- master_vec: float32 [6, 768], P(None, 'dp')
- first_qkv: float32 [768, 2304], P('dp')
- first_out: float32 [768, 768], P('dp')
- first_gu: float32 [768, 6144], P('dp')
- first_down: float32 [3072, 768], P('dp')
- first_vec: float32 [6, 768], P(None, 'dp')
- second_qkv: float32 [768, 2304], P('dp'), as said below
- second_out: float32 [768, 768], P('dp'), as said below
- second_gu: float32 [768, 6144], P('dp'), as said below
- second_down: float32 [3072, 768], P('dp'), as said below
- second_vec: float32 [6, 768], P(None, 'dp'), as said below
Outputs:
- output: bfloat16 [24576, 768], P(('dp', 'head'))
- grad_input: float32 [24576, 768], P(('dp', 'head'))
- new_qkv: float32 [768, 2304], P('dp')
- moment1_qkv: float32 [768, 2304], P('dp')
- moment2_qkv: float32 [768, 2304], P('dp')
- copy_qkv: bfloat16 [768, 2304], P('dp')
- new_out: float32 [768, 768], P('dp')
- moment1_out: float32 [768, 768], P('dp')
- moment2_out: float32 [768, 768], P('dp')
- copy_out: bfloat16 [768, 768], P('dp')
- new_gu: float32 [768, 6144], P('dp')
- moment1_gu: float32 [768, 6144], P('dp')
- moment2_gu: float32 [768, 6144], P('dp')
- copy_gu: bfloat16 [768, 6144], P('dp')
- new_down: float32 [3072, 768], P('dp')
- moment1_down: float32 [3072, 768], P('dp')
- moment2_down: float32 [3072, 768], P('dp')
- copy_down: bfloat16 [3072, 768], P('dp')
- new_vec: float32 [6, 768], P(None, 'dp')
- moment1_vec: float32 [6, 768], P(None, 'dp')
- moment2_vec: float32 [6, 768], P(None, 'dp')
- copy_vec: bfloat16 [6, 768], P(None, 'dp')
- grad_norm: float32 [1], replicated
Inputs may be any that keep to these rules, and one draw needn't show every extreme that they name: `segment_ids`: ids never fall; each aligned block of 1024 tokens holds whole sequences of 128, 256 or 512 tokens, and no id appears in two blocks; block k's ids lie within 8 * k to 8 * k + 5. `clip_norm`: Positive. `second_qkv`: Positive. `second_out`: Positive. `second_gu`: Positive. `second_down`: Positive. `second_vec`: Positive.
All inputs are finite; a program needn't handle non-finite values.
Results may differ from a plain program's by a relative error of at most 0.019.
The roundings to bfloat16 on the way count: a program that leaves them out, or rounds other values in their place, can miss the bound.
Values may be sent and summed in bfloat16 or wider, within the bound.
No kernel may reach another device: no remote copies, remote signals or barrier semaphores. Data moves between devices by JAX's collectives and lax.ppermute only.
A program may use at most 192 MiB of HBM per device.

v0:
```python
import jax
import jax.numpy as jnp
import numpy as np
from jax import lax
from jax.sharding import PartitionSpec as P

HEADS = 12
HEAD_DIM = 64
PACK = 1024
SLOPES = [2.0 ** (-(level + 1)) for level in range(8)] + [
    2.0 ** (-(level + 0.5)) for level in range(4)
]
LN_EPS = 1e-05
BETA_ONE = 0.9
BETA_TWO = 0.999
ADAM_EPS = 1e-08
CORR_ONE = 1.0 - 0.9**10
CORR_TWO = 1.0 - 0.999**10
RATE_MAT = 0.05
RATE_VEC = 0.5
DECAY_MAT = 0.01


def layer_norm(hidden, gain_vec, shift_vec):
    center = hidden - jnp.mean(hidden, axis=-1, keepdims=True)
    spread = jnp.mean(center * center, axis=-1, keepdims=True)
    return center * lax.rsqrt(spread + LN_EPS) * gain_vec + shift_vec


def gating(joined):
    half_width = joined.shape[-1] // 2
    return jax.nn.gelu(joined[:, :half_width], approximate=False) * joined[:, half_width:]


def contract_rows(left_rows, right_rows):
    return lax.dot_general(
        left_rows, right_rows, (((0,), (0,)), ((), ())), preferred_element_type=jnp.float32
    )


def times_transposed(left_rows, weight):
    return lax.dot_general(
        left_rows, weight, (((1,), (1,)), ((), ())), preferred_element_type=jnp.float32
    )


def adam_update(master, first_mom, second, grad_term, factor, step_rate, decay_rate):
    clipped = grad_term * factor
    first_new = BETA_ONE * first_mom + (1.0 - BETA_ONE) * clipped
    second_new = BETA_TWO * second + (1.0 - BETA_TWO) * clipped * clipped
    direction = first_new / CORR_ONE / (jnp.sqrt(second_new / CORR_TWO) + ADAM_EPS)
    master_new = master - step_rate * (direction + decay_rate * master)
    return (master_new, first_new, second_new, master_new.astype(jnp.bfloat16))


def pack_scores(queries, keys_part, seg_pack, slopes_local, score_scale):
    scores = (
        jnp.einsum("qhd,khd->hqk", queries, keys_part, preferred_element_type=jnp.float32)
        * score_scale
    )
    positions = jnp.arange(seg_pack.shape[0]).astype(jnp.float32)
    distance = jnp.abs(positions[:, None] - positions[None, :])
    same_seq = seg_pack[:, None] == seg_pack[None, :]
    return jnp.where(
        same_seq[None], scores - slopes_local[:, None, None] * distance[None], -1000000000.0
    )


def body(
    tokens,
    segment_ids,
    cotangent,
    clip_norm,
    master_qkv,
    master_out,
    master_gu,
    master_down,
    master_vec,
    first_qkv,
    first_out,
    first_gu,
    first_down,
    first_vec,
    second_qkv,
    second_out,
    second_gu,
    second_down,
    second_vec,
):
    groups = lax.axis_size("head")
    heads_local = HEADS // groups
    group_width = heads_local * HEAD_DIM
    tok_rows = tokens.shape[0]
    model_width = tokens.shape[1]
    score_scale = HEAD_DIM ** (-0.5)
    low_qkv = master_qkv.astype(jnp.bfloat16)
    low_out = master_out.astype(jnp.bfloat16)
    low_gu = master_gu.astype(jnp.bfloat16)
    low_down = master_down.astype(jnp.bfloat16)
    low_vec = master_vec.astype(jnp.bfloat16)
    full_qkv, full_out, full_gu, full_down, full_vec = (
        lax.all_gather(low_qkv, "dp", axis=0, tiled=True),
        lax.all_gather(low_out, "dp", axis=0, tiled=True),
        lax.all_gather(low_gu, "dp", axis=0, tiled=True),
        lax.all_gather(low_down, "dp", axis=0, tiled=True),
        lax.all_gather(low_vec, "dp", axis=1, tiled=True),
    )
    vectors = full_vec.astype(jnp.float32)
    slopes_local = lax.dynamic_slice_in_dim(
        jnp.asarray(np.array(SLOPES), jnp.float32),
        lax.axis_index("head") * heads_local,
        heads_local,
    )
    joined = jnp.dot(tokens, full_qkv, preferred_element_type=jnp.float32).astype(jnp.bfloat16)
    regrouped = lax.all_to_all(
        joined.reshape(tok_rows, 3, groups, group_width),
        "head",
        split_axis=2,
        concat_axis=0,
        tiled=True,
    )
    group_rows = regrouped.shape[0]
    pack_count = group_rows // PACK
    by_pack = regrouped.reshape(pack_count, PACK, 3, heads_local, HEAD_DIM)
    seg_packs = segment_ids.reshape(pack_count, PACK)

    def forward_pack(pieces):
        pack_block, seg_pack = pieces
        scores = pack_scores(
            pack_block[:, 0], pack_block[:, 1], seg_pack, slopes_local, score_scale
        )
        row_peak = jnp.max(scores, axis=-1, keepdims=True)
        exp_terms = jnp.exp(scores - row_peak)
        row_total = jnp.sum(exp_terms, axis=-1, keepdims=True)
        soft_weights = (exp_terms / row_total).astype(jnp.bfloat16)
        context = jnp.einsum(
            "hqk,khd->qhd", soft_weights, pack_block[:, 2], preferred_element_type=jnp.float32
        )
        return (
            context.astype(jnp.bfloat16).reshape(PACK, group_width),
            (row_peak + jnp.log(row_total))[..., 0],
        )

    context_packs, log_totals = lax.map(forward_pack, (by_pack, seg_packs))
    context_back = lax.all_to_all(
        context_packs.reshape(group_rows, 1, group_width),
        "head",
        split_axis=0,
        concat_axis=1,
        tiled=True,
    )
    context_rows = context_back.reshape(tok_rows, model_width)
    inputs = tokens.astype(jnp.float32)
    attn_out = jnp.dot(context_rows, full_out, preferred_element_type=jnp.float32)
    first_sum = inputs + attn_out + vectors[4]
    normed_one, norm_one_pull = jax.vjp(layer_norm, first_sum, vectors[0], vectors[1])
    normed_low = normed_one.astype(jnp.bfloat16)
    gate_up = jnp.dot(normed_low, full_gu, preferred_element_type=jnp.float32)
    hidden_full, gating_pull = jax.vjp(gating, gate_up)
    hidden_low = hidden_full.astype(jnp.bfloat16)
    ffn_out = jnp.dot(hidden_low, full_down, preferred_element_type=jnp.float32)
    second_sum = normed_one + ffn_out + vectors[5]
    result, norm_two_pull = jax.vjp(layer_norm, second_sum, vectors[2], vectors[3])
    grad_second, grad_gain_two, grad_shift_two = norm_two_pull(cotangent.astype(jnp.float32))
    grad_bias_down = jnp.sum(grad_second, axis=0)
    grad_ffn_low = grad_second.astype(jnp.bfloat16)
    grad_down = contract_rows(hidden_low, grad_ffn_low)
    grad_hidden = times_transposed(grad_ffn_low, full_down)
    (grad_joined_full,) = gating_pull(grad_hidden)
    grad_gate_up = grad_joined_full.astype(jnp.bfloat16)
    grad_gu = contract_rows(normed_low, grad_gate_up)
    grad_normed = grad_second + times_transposed(grad_gate_up, full_gu)
    grad_first, grad_gain_one, grad_shift_one = norm_one_pull(grad_normed)
    grad_bias_out = jnp.sum(grad_first, axis=0)
    grad_attn_low = grad_first.astype(jnp.bfloat16)
    grad_out = contract_rows(context_rows, grad_attn_low)
    grad_context = times_transposed(grad_attn_low, full_out).astype(jnp.bfloat16)
    grad_context_group = lax.all_to_all(
        grad_context.reshape(tok_rows, groups, group_width),
        "head",
        split_axis=1,
        concat_axis=0,
        tiled=True,
    )
    grad_packs = grad_context_group.reshape(pack_count, PACK, heads_local, HEAD_DIM)

    def backward_pack(pieces):
        pack_block, seg_pack, log_total, grad_ctx = pieces
        queries = pack_block[:, 0]
        keys_part = pack_block[:, 1]
        values_part = pack_block[:, 2]
        scores = pack_scores(queries, keys_part, seg_pack, slopes_local, score_scale)
        soft_full = jnp.exp(scores - log_total[..., None])
        grad_soft = jnp.einsum(
            "qhd,khd->hqk", grad_ctx, values_part, preferred_element_type=jnp.float32
        )
        grad_values = jnp.einsum(
            "hqk,qhd->khd",
            soft_full.astype(jnp.bfloat16),
            grad_ctx,
            preferred_element_type=jnp.float32,
        )
        row_inner = jnp.sum(soft_full * grad_soft, axis=-1, keepdims=True)
        grad_scores = (soft_full * (grad_soft - row_inner)).astype(jnp.bfloat16)
        grad_queries = (
            jnp.einsum("hqk,khd->qhd", grad_scores, keys_part, preferred_element_type=jnp.float32)
            * score_scale
        )
        grad_keys = (
            jnp.einsum("hqk,qhd->khd", grad_scores, queries, preferred_element_type=jnp.float32)
            * score_scale
        )
        stacked = jnp.stack((grad_queries, grad_keys, grad_values), axis=1).astype(jnp.bfloat16)
        return stacked.reshape(PACK, 3, group_width)

    grad_blocks = lax.map(backward_pack, (by_pack, seg_packs, log_totals, grad_packs))
    grad_joined = lax.all_to_all(
        grad_blocks.reshape(group_rows, 3, 1, group_width),
        "head",
        split_axis=0,
        concat_axis=2,
        tiled=True,
    )
    grad_joined_rows = grad_joined.reshape(tok_rows, 3 * model_width)
    grad_qkv = contract_rows(tokens, grad_joined_rows)
    grad_input = grad_first + times_transposed(grad_joined_rows, full_qkv)
    grad_vec = jnp.stack(
        (
            grad_gain_one,
            grad_shift_one,
            grad_gain_two,
            grad_shift_two,
            grad_bias_out,
            grad_bias_down,
        )
    )
    shard_qkv, shard_out, shard_gu, shard_down, shard_vec = (
        lax.psum_scatter(grad_qkv, "dp", scatter_dimension=0, tiled=True),
        lax.psum_scatter(grad_out, "dp", scatter_dimension=0, tiled=True),
        lax.psum_scatter(grad_gu, "dp", scatter_dimension=0, tiled=True),
        lax.psum_scatter(grad_down, "dp", scatter_dimension=0, tiled=True),
        lax.psum_scatter(grad_vec, "dp", scatter_dimension=1, tiled=True),
    )
    shards = (
        lax.psum(shard_qkv.astype(jnp.bfloat16), "head").astype(jnp.float32),
        lax.psum(shard_out.astype(jnp.bfloat16), "head").astype(jnp.float32),
        lax.psum(shard_gu.astype(jnp.bfloat16), "head").astype(jnp.float32),
        lax.psum(shard_down.astype(jnp.bfloat16), "head").astype(jnp.float32),
        lax.psum(shard_vec.astype(jnp.bfloat16), "head").astype(jnp.float32),
    )
    squares = jnp.float32(0.0)
    for shard_piece in shards:
        squares = squares + jnp.sum(shard_piece * shard_piece)
    grad_norm = jnp.sqrt(lax.psum(squares, "dp"))
    factor = jnp.minimum(1.0, clip_norm[0] / grad_norm)
    up_qkv = adam_update(master_qkv, first_qkv, second_qkv, shards[0], factor, RATE_MAT, DECAY_MAT)
    up_out = adam_update(master_out, first_out, second_out, shards[1], factor, RATE_MAT, DECAY_MAT)
    up_gu = adam_update(master_gu, first_gu, second_gu, shards[2], factor, RATE_MAT, DECAY_MAT)
    up_down = adam_update(
        master_down, first_down, second_down, shards[3], factor, RATE_MAT, DECAY_MAT
    )
    up_vec = adam_update(master_vec, first_vec, second_vec, shards[4], factor, RATE_VEC, 0.0)
    return (
        result.astype(jnp.bfloat16),
        grad_input,
        up_qkv[0],
        up_qkv[1],
        up_qkv[2],
        up_qkv[3],
        up_out[0],
        up_out[1],
        up_out[2],
        up_out[3],
        up_gu[0],
        up_gu[1],
        up_gu[2],
        up_gu[3],
        up_down[0],
        up_down[1],
        up_down[2],
        up_down[3],
        up_vec[0],
        up_vec[1],
        up_vec[2],
        up_vec[3],
        grad_norm.reshape(1),
    )


def solution(mesh):
    in_specs = (
        P(("dp", "head"), None),
        P("dp"),
        P(("dp", "head"), None),
        P(),
        P("dp", None),
        P("dp", None),
        P("dp", None),
        P("dp", None),
        P(None, "dp"),
        P("dp", None),
        P("dp", None),
        P("dp", None),
        P("dp", None),
        P(None, "dp"),
        P("dp", None),
        P("dp", None),
        P("dp", None),
        P("dp", None),
        P(None, "dp"),
    )
    out_specs = (
        P(("dp", "head"), None),
        P(("dp", "head"), None),
        P("dp", None),
        P("dp", None),
        P("dp", None),
        P("dp", None),
        P("dp", None),
        P("dp", None),
        P("dp", None),
        P("dp", None),
        P("dp", None),
        P("dp", None),
        P("dp", None),
        P("dp", None),
        P("dp", None),
        P("dp", None),
        P("dp", None),
        P("dp", None),
        P(None, "dp"),
        P(None, "dp"),
        P(None, "dp"),
        P(None, "dp"),
        P(),
    )
    return jax.shard_map(body, mesh=mesh, in_specs=in_specs, out_specs=out_specs, check_vma=False)
```

profile of v0, /device:TPU:0, one launch (start us, length us, event | category | flops | bytes accessed | tf_op | source)
XLA Modules:
  0.0 1466.3 jit_solution(240032955310916540)
XLA Ops:
  9.2 69.5 %all-gather.6.cloned.1.call-done = bf16[768,2304]{1,0:T(8,128)(2,1)} async-done(((bf16[96,2304]{1,0:T(8,128)(2,1)}), bf16[768,2304]{1,0:T(8,128)(2,1)}) %all-gather.6.cloned.1.call-update) | async-done | bytes 3538960 | tf_op jit(solution)/shard_map/all_gather | solution.py:102
  102.7 34.4 %all-to-all-done = bf16[768,3,4,192]{0,3,1,2:T(8,128)(2,1)S(1)} async-done(((bf16[768,3,4,192]{0,3,1,2:T(8,128)(2,1)}), bf16[768,3,4,192]{0,3,1,2:T(8,128)(2,1)S(1)}, u32[]{:S(2)}, u32[]{:S(2)}) %all-to-all-start) | async-done | bytes 3538976 | tf_op jit(solution)/shard_map/all_to_all | solution.py:115
  141.6 10.9 reshape.363
  156.2 45.1 %while.22 = (s32[]{:T(128)}, bf16[3,1024,192]{1,2,0:T(8,128)(2,1)}, f32[3,3,1024]{2,1,0:T(4,128)}, bf16[3,1024,3,3,64]{1,4,3,2,0:T(8,128)(2,1)S(1)}, s32[3,1024]{1,0:T(4,128)S(1)}, /*index=5*/f32[3]{0:T(128)}, s32[]{:T(128)}) while((s32[]{:T(128)}, bf16[3,1024,192]{1,2,0:T(8,128)(2,1)}, f32[3,3,1024]{2,1,0:T(4,128)}, ...), condition=%wide.region_3.4_spmd, body=%wide.region_0.3_spmd.sunk | while | flops 865269760 | bytes 63571132 | solution.py:144
  203.8 10.0 reshape.379
  214.4 19.5 %reduce.12 = bf16[3072,192]{1,0:T(8,128)(2,1)} reduce(bf16[3072,1,192]{2,1,0:T(2,128)(2,1)} %reshape.379, bf16[]{:T(256)} %broadcast.241), dimensions={1}, to_apply=%reshape.379.reduce_sub_computation | reduce | bytes 2359298 | tf_op jit(solution)/shard_map/reshape | solution.py:146
  249.5 26.2 %all-gather = bf16[8,96,6]{1,2,0:T(8,128)(2,1)S(1)} all-gather(bf16[1,96,6]{1,2,0:T(8,128)(2,1)S(1)} %convert_bitcast_fusion), channel_id=1, replica_groups=mesh['dp'=8,'head'=4] {'dp'}, dimensions={0}, use_global_device_ids=true | all-gather | bytes 10368 | tf_op jit(solution)/shard_map/all_gather | solution.py:106
  284.1 7.3 copy.135
  302.8 11.6 fusion.63
  321.2 21.9 %multiply_convert_fusion.1 = (bf16[768,3072]{1,0:T(8,128)(2,1)}, f32[768,3072]{1,0:T(8,128)}) fusion(f32[768,6144]{1,0:T(8,128)S(1)} %fusion.63), kind=kLoop, calls=%fused_computation.51 | loop fusion | flops 155713536 | bytes 33030144 | tf_op jit(solution)/shard_map/convert_element_type | solution.py:160
  343.1 17.3 %all-gather.12.cloned.1.call-done = bf16[3072,768]{1,0:T(8,128)(2,1)} async-done(((bf16[384,768]{1,0:T(8,128)(2,1)}), bf16[3072,768]{1,0:T(8,128)(2,1)}) %all-gather.12.cloned.1.call-update) | async-done | bytes 4718608 | tf_op jit(solution)/shard_map/all_gather | solution.py:105
  360.3 9.0 fusion.84
  374.9 18.9 %fusion.28 = (f32[768,3072]{1,0:T(8,128)}, f32[768,3072]{1,0:T(8,128)}) fusion(f32[768,3072]{1,0:T(8,128)} %get-tuple-element.294, f32[768,6144]{1,0:T(8,128)} %copy-done, bf16[3072,768]{1,0:T(8,128)(2,1)} %all-gather.12.cloned.1.call-done, f32[768,768]{0,1:T(8,128)} %get-tuple-element.292, f32[768]{0:T(1024)S(1)} %negate_multiply_fusion.2), kind=kOutput, calls=%fused_computation.75 | convolution fusion | flops 3662807040 | bytes 54266880 | tf_op jit(solution)/shard_map/dot_general | solution.py:42
  393.8 19.8 %multiply_reduce_fusion.1 = (f32[768]{0:T(1024)}, f32[768]{0:T(1024)}, f32[768]{0:T(1024)}, f32[768,768]{0,1:T(8,128)}) fusion(f32[768,768]{0,1:T(8,128)} %copy-done.3, f32[768]{0:T(1024)S(1)} %fusion.58, f32[768]{0:T(1024)S(1)} %broadcast_multiply_fusion.1, f32[768]{0:T(1024)S(1)} %get-tuple-element.237, ...), kind=kOutput, calls=%fused_computation.87 | convolution fusion | flops 7263089664 | bytes 35410944 | tf_op jit(solution)/shard_map/dot_general | solution.py:42
  428.6 11.2 all-to-all-done.2
  450.5 95.2 %while.23 = (s32[]{:T(128)}, bf16[3,1024,3,192]{1,3,2,0:T(8,128)(2,1)}, bf16[3,1024,3,3,64]{1,4,3,2,0:T(8,128)(2,1)S(1)}, s32[3,1024]{1,0:T(4,128)}, f32[3]{0:T(...) while((s32[]{:T(128)}, bf16[3,1024,3,192]{1,3,2,0:T(8,128)(2,1)}, ...), condition=%wide.region_14.15_spmd, body=%wide.region_12.14_spmd.sunk | while | flops 2055534592 | bytes 141906608 | solution.py:216
  456.2 8.2 multiply_reduce_fusion.6
  488.0 8.2 multiply_reduce_fusion.6
  519.7 8.2 multiply_reduce_fusion.6
  545.6 9.8 copy.165
  555.5 77.7 %all_to_all.60 = bf16[3072,3,1,192]{3,1,2,0:T(4,128)(2,1)} all-to-all(bf16[3072,3,1,192]{3,1,2,0:T(4,128)(2,1)} %bitcast.155), channel_id=1, replica_groups=mesh['dp'=8,'head'=4] {'head'}, dimensions={0} | all-to-all | bytes 7077888 | tf_op jit(solution)/shard_map/all_to_all | solution.py:217
  633.2 10.5 copy.166
  651.0 8.0 copy.167
  660.7 8.8 fusion.47
  671.2 20.7 %fusion.40 = f32[768,6144]{1,0:T(8,128)} fusion(f32[768,3072]{1,0:T(8,128)} %get-tuple-element.300, f32[768,3072]{1,0:T(8,128)} %get-tuple-element.299, f32[768,768]{0,1:T(8,128)S(1)} %copy-done.4, f32[768]{0:T(1024)S(1)} %copy-done.31, f32[768]{0:T(1024)S(1)} %copy-done.29, f32[768]{0:T(1024)S(1)} %copy-done.27, f32[768]{0:T(1024)S(1)} %copy-done.25), kind=kOutput, calls=%fused_computation.111 | convolution fusion | flops 7260143616 | bytes 40120320 | tf_op jit(solution)/shard_map/dot_general | solution.py:36
  697.4 88.2 %reduce-scatter.16.cloned.1.call-done = f32[96,2304]{1,0:T(8,128)} async-done(((f32[768,2304]{1,0:T(8,128)}), f32[96,2304]{1,0:T(8,128)}) %reduce-scatter.16.cloned.1.call-update) | async-done | bytes 884752
  787.7 164.3 %reduce-scatter.14.cloned.1.call-done = f32[384,768]{1,0:T(8,128)} async-done(((f32[3072,768]{1,0:T(8,128)}), f32[384,768]{1,0:T(8,128)}) %reduce-scatter.14.cloned.1.call-update) | async-done | bytes 1179664 | tf_op jit(solution)/shard_map/reduce_scatter | solution.py:241
  954.2 314.8 %reduce-scatter.12.cloned.1.call-done = f32[96,6144]{1,0:T(8,128)} async-done(((f32[768,6144]{1,0:T(8,128)}), f32[96,6144]{1,0:T(8,128)}) %reduce-scatter.12.cloned.1.call-update) | async-done | bytes 2359312 | tf_op jit(solution)/shard_map/reduce_scatter | solution.py:240
  1280.5 53.2 %reduce-scatter.18.cloned.1.call-done = f32[96,6]{1,0:T(8,128)} async-done(((f32[768,6]{1,0:T(8,128)}), f32[96,6]{1,0:T(8,128)}) %reduce-scatter.18.cloned.1.call-update) | async-done | bytes 2320
  1341.0 7.9 add_add_fusion.4
  1348.8 47.1 %all-reduce.5.cloned.1.call-done = (bf16[96,2304]{0,1:T(8,128)(2,1)}, bf16[96,768]{1,0:T(8,128)(2,1)}, bf16[96,6144]{1,0:T(8,128)(2,1)}, bf16[384,768]{1,0:T(8,128)(2,1)}) async-done(((bf16[96,2304]{0,1:T(8,128)(2,1)}, bf16[96,768]{1,0:T(8,128)(2,1)}, bf16[96,6144]{1,0:T(8,128)(2,1)}, bf16[384,768]{1,0:T(8,128)(2,1)}), (bf16[96,2304]{0,1:T(8,128)(2,1)}, bf16[96,768]{1,0:T(8,128)(2,1)}, ...) | async-done | bytes 2359312 | tf_op jit(solution)/shard_map/psum | solution.py:245
  1410.4 21.8 %psum.47 = f32[]{:T(128)} all-reduce(f32[]{:T(128)S(6)} %add.231), channel_id=1, replica_groups=mesh['dp'=8,'head'=4] {'dp'}, use_global_device_ids=true, to_apply=%region_36.37 | all-reduce | flops 1 | bytes 8 | tf_op jit(solution)/shard_map/psum | solution.py:254
  (291 shorter events, 300.5 us)
Async XLA Ops:
  7.2 71.5 %all-gather.6.cloned.1.call-start = ((), (), s32[]{:S(2)}) async-start(), calls=%async_computation.9 | async-start | bytes 3981312 | tf_op jit(solution)/shard_map/all_gather | solution.py:102
  92.3 44.9 %all-to-all-start = ((bf16[768,3,4,192]{0,3,1,2:T(8,128)(2,1)}), bf16[768,3,4,192]{0,3,1,2:T(8,128)(2,1)S(1)}, u32[]{:S(2)}, u32[]{:S(2)}) async-start(bf16[768,3,4,192]{0,3,1,2:T(8,128)(2,1)} %copy.130), calls=%async_computation | async-start | bytes 7077888 | tf_op jit(solution)/shard_map/all_to_all | solution.py:115
  96.0 201.2 %all-gather.8.cloned.1.call-start = ((), (), s32[]{:S(2)}) async-start(), calls=%async_computation.10 | async-start | bytes 1327104 | tf_op jit(solution)/shard_map/all_gather | solution.py:103
  97.7 205.1 %all-gather.10.cloned.1.call-start = ((), (), s32[]{:S(2)}) async-start(), calls=%async_computation.11 | async-start | bytes 10616832 | tf_op jit(solution)/shard_map/all_gather | solution.py:104
  201.3 12.5 copy-start.32
  238.2 41.1 %all-to-all-start.1 = ((bf16[4,2,73728]{2,1,0:T(2,128)(2,1)}), bf16[4,2,73728]{2,1,0:T(2,128)(2,1)}, u32[]{:S(2)}, u32[]{:S(2)}) async-start(bf16[4,2,73728]{2,1,0:T(2,128)(2,1)} %reshape.390), calls=%async_computation.1 | async-start | bytes 2359296 | tf_op jit(solution)/shard_map/all_to_all | solution.py:145
  242.5 117.8 %all-gather.12.cloned.1.call-start = ((), (), s32[]{:S(2)}) async-start(), calls=%async_computation.12 | async-start | bytes 5308416 | tf_op jit(solution)/shard_map/all_gather | solution.py:105
  279.3 81.0 %copy-start.30 = (f32[768]{0:T(1024)}, f32[768]{0:T(1024)S(1)}, u32[]{:S(2)}) copy-start(f32[768]{0:T(1024)S(1)} %get-tuple-element.236) | copy-start | bytes 9220
  279.3 135.0 %copy-start.28 = (f32[768]{0:T(1024)}, f32[768]{0:T(1024)S(1)}, u32[]{:S(2)}) copy-start(f32[768]{0:T(1024)S(1)} %get-tuple-element.237) | copy-start | bytes 9220
  300.5 113.8 %copy-start.24 = (f32[768]{0:T(1024)}, f32[768]{0:T(1024)S(1)}, u32[]{:S(2)}) copy-start(f32[768]{0:T(1024)S(1)} %broadcast_multiply_fusion.1) | copy-start | bytes 9220
  302.8 111.5 %copy-start.26 = (f32[768]{0:T(1024)}, f32[768]{0:T(1024)S(1)}, u32[]{:S(2)}) copy-start(f32[768]{0:T(1024)S(1)} %fusion.58) | copy-start | bytes 9220
  314.4 6.8 copy-start
  374.9 18.9 %copy-start.42 = (f32[768]{0:T(1024)}, f32[768]{0:T(1024)S(1)}, u32[]{:S(2)}) copy-start(f32[768]{0:T(1024)S(1)} %negate_multiply_fusion.2) | copy-start | bytes 9220
  393.8 19.8 %copy-start.37 = (f32[768]{0:T(1024)S(1)}, f32[768]{0:T(1024)}, u32[]{:S(2)}) copy-start(f32[768]{0:T(1024)} %copy-done.36) | copy-start | bytes 9220
  419.6 20.2 %all-to-all-start.2 = ((bf16[768,4,192]{0,2,1:T(8,128)(2,1)}), bf16[768,4,192]{0,2,1:T(8,128)(2,1)}, u32[]{:S(2)}, u32[]{:S(2)}) async-start(bf16[768,4,192]{0,2,1:T(8,128)(2,1)} %bitcast.167), calls=%async_computation.2 | async-start | bytes 2359296 | tf_op jit(solution)/shard_map/all_to_all | solution.py:178
  423.9 271.8 %reduce-scatter.10.cloned.1.call-start = ((), (), s32[]{:S(2)}) async-start(), calls=%async_computation.13 | async-start | bytes 2654208 | tf_op jit(solution)/shard_map/reduce_scatter | solution.py:239
  428.6 357.0 %reduce-scatter.16.cloned.1.call-start = ((), (), s32[]{:S(2)}) async-start(), calls=%async_computation.16 | async-start | bytes 7962624
  443.0 7.4 copy-start.34
  659.1 293.0 %reduce-scatter.14.cloned.1.call-start = ((), (), s32[]{:S(2)}) async-start(), calls=%async_computation.15 | async-start | bytes 10616832 | tf_op jit(solution)/shard_map/reduce_scatter | solution.py:241
  669.6 599.4 %reduce-scatter.12.cloned.1.call-start = ((), (), s32[]{:S(2)}) async-start(), calls=%async_computation.14 | async-start | bytes 21233664 | tf_op jit(solution)/shard_map/reduce_scatter | solution.py:240
  692.0 641.7 %reduce-scatter.18.cloned.1.call-start = ((), (), s32[]{:S(2)}) async-start(), calls=%async_computation.17 | async-start | bytes 442368
  695.6 700.2 %all-reduce.5.cloned.1.call-start = ((), (), s32[]{:S(2)}) async-start(), calls=%async_computation.18 | async-start | bytes 5013504 | tf_op jit(solution)/shard_map/psum | solution.py:245
  954.2 317.6 %copy-start.19 = (f32[96,2304]{1,0:T(8,128)S(1)}, f32[96,2304]{1,0:T(8,128)}, u32[]{:S(2)}) copy-start(f32[96,2304]{1,0:T(8,128)} %param.28) | copy-start | bytes 2654212
  1407.1 25.8 %copy-start.14 = (f32[96,2304]{0,1:T(8,128)S(1)}, f32[96,2304]{0,1:T(8,128)}, u32[]{:S(2)}) copy-start(f32[96,2304]{0,1:T(8,128)} %copy.151) | copy-start | bytes 2654212
  1407.2 25.8 %copy-start.15 = (f32[96,2304]{0,1:T(8,128)S(1)}, f32[96,2304]{0,1:T(8,128)}, u32[]{:S(2)}) copy-start(f32[96,2304]{0,1:T(8,128)} %copy.148) | copy-start | bytes 2654212
  1407.2 25.8 %copy-start.16 = (f32[96,2304]{0,1:T(8,128)S(1)}, f32[96,2304]{0,1:T(8,128)}, u32[]{:S(2)}) copy-start(f32[96,2304]{0,1:T(8,128)} %copy.149) | copy-start | bytes 2654212
  1440.6 7.1 copy-start.6
  1440.6 7.1 copy-start.11
  1447.7 7.2 copy-start.12
  1447.7 7.2 copy-start.20
  1447.7 7.1 copy-start.22
  1447.7 7.1 copy-start.23
  (39 other events, 84.2 us)
Sparse Core Ops, SparseCore 0:
  10.8 67.8 all-gather.5
  99.6 40.1 all-gather.7
  142.5 136.8 all-gather.9
  282.0 78.2 all-gather.11
  428.7 67.6 reduce-scatter.9
  659.2 126.2 reduce-scatter.15
  789.5 162.4 reduce-scatter.13
  956.4 312.4 reduce-scatter.11
  1273.1 60.4 reduce-scatter.17
  1338.0 57.7 all-reduce.4
where the time goes:
time: 1480 us; the launch traced here: 1470 us
  waiting for transfers between devices  800 us (54%)
  matrix products  208 us (14%)
  local copies, waits for them, and re-layouts  159 us (11%)
  other arithmetic  134 us (9%)
  blocking collectives  132 us (9%)
  between operations  20.8 us (1%)
    reduce_scatter x1, waiting for transfers between devices, body(): lax.psum_scatter(grad_gu, 'dp', scatter_dimension=0, tiled=True)  315 us
    reduce_scatter x1, waiting for transfers between devices, body(): lax.psum_scatter(grad_down, 'dp', scatter_dimension=0, tiled=True)  164 us
    unnamed x12, waiting for transfers between devices  141 us
    all_to_all x1, blocking collectives, body(): lax.all_to_all(grad_blocks.reshape(group_rows, 3, 1, group_width), 'head'...  77.7 us
    all_gather x1, waiting for transfers between devices, body(): lax.all_gather(low_qkv, 'dp', axis=0, tiled=True)  69.5 us
    unnamed x115, local copies, waits for them, and re-layouts  62.8 us
    dot_general x4, matrix products, times_transposed(): lax.dot_general(left_rows, weight, (((1,), (1,)), ((), ())), preferred_el...  48.7 us
    psum x1, waiting for transfers between devices, body(): lax.psum(shard_qkv.astype(jnp.bfloat16), 'head').astype(jnp.float32)  47.1 us
  transfers between devices with their start and end apart: 13, of which 9 were waited for; matrix products, arithmetic and copies ran while one was open for 25% of the time, Pallas kernels for 0%

commit v1 on v0

--- a/solution.py
+++ b/solution.py
@@ -242,7 +242,7 @@
         lax.psum_scatter(grad_vec, "dp", scatter_dimension=1, tiled=True),
     )
     shards = (
-        lax.psum(shard_qkv.astype(jnp.bfloat16), "head").astype(jnp.float32),
+        jnp.sum(lax.all_gather(shard_qkv.astype(jnp.bfloat16), "head"), axis=0).astype(jnp.float32),
         lax.psum(shard_out.astype(jnp.bfloat16), "head").astype(jnp.float32),
         lax.psum(shard_gu.astype(jnp.bfloat16), "head").astype(jnp.float32),
         lax.psum(shard_down.astype(jnp.bfloat16), "head").astype(jnp.float32),

time: 1480 us -> 1550 us (1.047)
  waiting for transfers between devices: 800 us -> 889 us
    reduce_scatter x0 -> x1, waiting for transfers between devices: none -> 84.4 us  [body(): lax.psum_scatter(grad_qkv, 'dp', scatter_dimension=0, tiled=True)]
    unnamed x12, waiting for transfers between devices: 141 us -> 60.5 us
    reduce_scatter x1, waiting for transfers between devices: 0.02 us -> 65.3 us  [body(): lax.psum_scatter(grad_out, 'dp', scatter_dimension=0, tiled=True)]
    unnamed x115, local copies, waits for them, and re-layouts: 62.8 us -> 44.7 us
  transfers between devices with their start and end apart: 13 -> 14, of which waited for: 9 -> 11; matrix products, arithmetic and copies ran while one was open for 25% -> 15% of each run, Pallas kernels for 0% -> 0%
where the time goes in v1:
time: 1550 us; the launch traced here: 1540 us
  waiting for transfers between devices  889 us (57%)
  matrix products  206 us (13%)
  local copies, waits for them, and re-layouts  144 us (9%)
  other arithmetic  133 us (9%)
  blocking collectives  132 us (9%)
  between operations  20.4 us (1%)
    reduce_scatter x1, waiting for transfers between devices, body(): lax.psum_scatter(grad_gu, 'dp', scatter_dimension=0, tiled=True)  315 us
    reduce_scatter x1, waiting for transfers between devices, body(): lax.psum_scatter(grad_down, 'dp', scatter_dimension=0, tiled=True)  165 us
    reduce_scatter x1, waiting for transfers between devices, body(): lax.psum_scatter(grad_qkv, 'dp', scatter_dimension=0, tiled=True)  84.4 us
    all_to_all x1, blocking collectives, body(): lax.all_to_all(grad_blocks.reshape(group_rows, 3, 1, group_width), 'head'...  77.7 us
    all_gather x1, waiting for transfers between devices, body(): lax.all_gather(low_qkv, 'dp', axis=0, tiled=True)  69.5 us
    reduce_scatter x1, waiting for transfers between devices, body(): lax.psum_scatter(grad_out, 'dp', scatter_dimension=0, tiled=True)  65.3 us
    unnamed x12, waiting for transfers between devices  60.5 us
    psum x1, waiting for transfers between devices, body(): lax.psum(shard_out.astype(jnp.bfloat16), 'head').astype(jnp.float32)  50.4 us
  transfers between devices with their start and end apart: 14, of which 11 were waited for; matrix products, arithmetic and copies ran while one was open for 15% of the time, Pallas kernels for 0%

profile of v1, /device:TPU:0, one launch (start us, length us, event | category | flops | bytes accessed | tf_op | source)
XLA Modules:
  0.0 1537.1 jit_solution(1415376190136189389)
XLA Ops:
  9.2 69.5 %all-gather.8.cloned.1.call-done = bf16[768,2304]{1,0:T(8,128)(2,1)} async-done(((bf16[96,2304]{1,0:T(8,128)(2,1)}), bf16[768,2304]{1,0:T(8,128)(2,1)}) %all-gather.8.cloned.1.call-update) | async-done | bytes 3538960 | tf_op jit(solution)/shard_map/all_gather | solution.py:102
  102.7 34.5 %all-to-all-done = bf16[768,3,4,192]{0,3,1,2:T(8,128)(2,1)S(1)} async-done(((bf16[768,3,4,192]{0,3,1,2:T(8,128)(2,1)}), bf16[768,3,4,192]{0,3,1,2:T(8,128)(2,1)S(1)}, u32[]{:S(2)}, u32[]{:S(2)}) %all-to-all-start) | async-done | bytes 3538976 | tf_op jit(solution)/shard_map/all_to_all | solution.py:115
  141.8 10.9 reshape.363
  156.5 45.1 %while.22 = (s32[]{:T(128)}, bf16[3,1024,192]{1,2,0:T(8,128)(2,1)}, f32[3,3,1024]{2,1,0:T(4,128)}, bf16[3,1024,3,3,64]{1,4,3,2,0:T(8,128)(2,1)S(1)}, s32[3,1024]{1,0:T(4,128)S(1)}, /*index=5*/f32[3]{0:T(128)}, s32[]{:T(128)}) while((s32[]{:T(128)}, bf16[3,1024,192]{1,2,0:T(8,128)(2,1)}, f32[3,3,1024]{2,1,0:T(4,128)}, ...), condition=%wide.region_3.4_spmd, body=%wide.region_0.3_spmd.sunk | while | flops 865269760 | bytes 63571132 | solution.py:144
  204.1 10.0 reshape.380
  214.6 19.5 %reduce.13 = bf16[3072,192]{1,0:T(8,128)(2,1)} reduce(bf16[3072,1,192]{2,1,0:T(2,128)(2,1)} %reshape.380, bf16[]{:T(256)} %broadcast.241), dimensions={1}, to_apply=%reshape.380.reduce_sub_computation | reduce | bytes 2359298 | tf_op jit(solution)/shard_map/reshape | solution.py:146
  249.8 26.1 %all-gather.1 = bf16[8,96,6]{1,2,0:T(8,128)(2,1)S(1)} all-gather(bf16[1,96,6]{1,2,0:T(8,128)(2,1)S(1)} %convert_bitcast_fusion), channel_id=1, replica_groups=mesh['dp'=8,'head'=4] {'dp'}, dimensions={0}, use_global_device_ids=true | all-gather | bytes 10368 | tf_op jit(solution)/shard_map/all_gather | solution.py:106
  303.0 11.6 fusion.63
  321.4 21.9 %multiply_convert_fusion.1 = (bf16[768,3072]{1,0:T(8,128)(2,1)}, f32[768,3072]{1,0:T(8,128)}) fusion(f32[768,6144]{1,0:T(8,128)S(1)} %fusion.63), kind=kLoop, calls=%fused_computation.51 | loop fusion | flops 155713536 | bytes 33030144 | tf_op jit(solution)/shard_map/convert_element_type | solution.py:160
  343.3 17.2 %all-gather.14.cloned.1.call-done = bf16[3072,768]{1,0:T(8,128)(2,1)} async-done(((bf16[384,768]{1,0:T(8,128)(2,1)}), bf16[3072,768]{1,0:T(8,128)(2,1)}) %all-gather.14.cloned.1.call-update) | async-done | bytes 4718608 | tf_op jit(solution)/shard_map/all_gather | solution.py:105
  360.5 9.0 fusion.84
  375.1 19.0 %fusion.28 = (f32[768,3072]{1,0:T(8,128)}, f32[768,3072]{1,0:T(8,128)}) fusion(f32[768,3072]{1,0:T(8,128)} %get-tuple-element.293, f32[768,6144]{1,0:T(8,128)} %copy-done, bf16[3072,768]{1,0:T(8,128)(2,1)} %all-gather.14.cloned.1.call-done, f32[768,768]{0,1:T(8,128)} %get-tuple-element.291, f32[768]{0:T(1024)S(1)} %negate_multiply_fusion.2), kind=kOutput, calls=%fused_computation.75 | convolution fusion | flops 3662807040 | bytes 54266880 | tf_op jit(solution)/shard_map/dot_general | solution.py:42
  394.1 19.8 %multiply_reduce_fusion.1 = (f32[768]{0:T(1024)}, f32[768]{0:T(1024)}, f32[768]{0:T(1024)}, f32[768,768]{0,1:T(8,128)}) fusion(f32[768,768]{0,1:T(8,128)} %copy-done.3, f32[768]{0:T(1024)S(1)} %fusion.58, f32[768]{0:T(1024)S(1)} %broadcast_multiply_fusion.1, f32[768]{0:T(1024)S(1)} %get-tuple-element.237, ...), kind=kOutput, calls=%fused_computation.87 | convolution fusion | flops 7263089664 | bytes 35410944 | tf_op jit(solution)/shard_map/dot_general | solution.py:42
  424.2 15.9 %all-to-all-done.2 = bf16[768,4,192]{0,2,1:T(8,128)(2,1)} async-done(((bf16[768,4,192]{0,2,1:T(8,128)(2,1)}), bf16[768,4,192]{0,2,1:T(8,128)(2,1)}, u32[]{:S(2)}, u32[]{:S(2)}) %all-to-all-start.2) | async-done | bytes 1179680 | tf_op jit(solution)/shard_map/all_to_all | solution.py:178
  450.7 95.0 %while.23 = (s32[]{:T(128)}, bf16[3,1024,3,192]{1,3,2,0:T(8,128)(2,1)}, bf16[3,1024,3,3,64]{1,4,3,2,0:T(8,128)(2,1)S(1)}, s32[3,1024]{1,0:T(4,128)}, f32[3]{0:T(...) while((s32[]{:T(128)}, bf16[3,1024,3,192]{1,3,2,0:T(8,128)(2,1)}, ...), condition=%wide.region_14.15_spmd, body=%wide.region_12.14_spmd.sunk | while | flops 2055534592 | bytes 141906608 | solution.py:216
  456.4 8.2 multiply_reduce_fusion.6
  488.0 8.2 multiply_reduce_fusion.6
  519.7 8.2 multiply_reduce_fusion.6
  545.7 9.8 copy.136
  555.5 77.7 %all_to_all.60 = bf16[3072,3,1,192]{3,1,2,0:T(4,128)(2,1)} all-to-all(bf16[3072,3,1,192]{3,1,2,0:T(4,128)(2,1)} %bitcast.156), channel_id=1, replica_groups=mesh['dp'=8,'head'=4] {'head'}, dimensions={0} | all-to-all | bytes 7077888 | tf_op jit(solution)/shard_map/all_to_all | solution.py:217
  633.3 10.5 copy.137
  651.1 8.1 copy.138
  670.1 8.8 fusion.47
  680.5 20.6 %fusion.39 = f32[768,6144]{1,0:T(8,128)} fusion(f32[768,3072]{1,0:T(8,128)} %get-tuple-element.299, f32[768,3072]{1,0:T(8,128)} %get-tuple-element.298, f32[768,768]{0,1:T(8,128)S(1)} %copy-done.4, f32[768]{0:T(1024)S(1)} %copy-done.34, f32[768]{0:T(1024)S(1)} %copy-done.32, f32[768]{0:T(1024)S(1)} %copy-done.30, f32[768]{0:T(1024)S(1)} %copy-done.26), kind=kOutput, calls=%fused_computation.107 | convolution fusion | flops 7260143616 | bytes 40120320 | tf_op jit(solution)/shard_map/dot_general | solution.py:36
  701.3 84.4 %reduce-scatter.16.cloned.1.call-done = f32[96,2304]{1,0:T(8,128)} async-done(((f32[768,2304]{1,0:T(8,128)}), f32[96,2304]{1,0:T(8,128)}) %reduce-scatter.16.cloned.1.call-update) | async-done | bytes 884752 | tf_op jit(solution)/shard_map/reduce_scatter | solution.py:238
  789.9 60.4 %reduce-scatter.18.cloned.1.call-done = f32[96,6]{1,0:T(8,128)} async-done(((f32[768,6]{1,0:T(8,128)}), f32[96,6]{1,0:T(8,128)}) %reduce-scatter.18.cloned.1.call-update) | async-done | bytes 2320
  857.5 65.3 %reduce-scatter.10.cloned.1.call-done = f32[96,768]{1,0:T(8,128)} async-done(((f32[768,768]{1,0:T(8,128)}), f32[96,768]{1,0:T(8,128)}) %reduce-scatter.10.cloned.1.call-update) | async-done | bytes 294928 | tf_op jit(solution)/shard_map/reduce_scatter | solution.py:239
  924.4 164.8 %reduce-scatter.14.cloned.1.call-done = f32[384,768]{1,0:T(8,128)} async-done(((f32[3072,768]{1,0:T(8,128)}), f32[384,768]{1,0:T(8,128)}) %reduce-scatter.14.cloned.1.call-update) | async-done | bytes 1179664 | tf_op jit(solution)/shard_map/reduce_scatter | solution.py:241
  1091.3 314.6 %reduce-scatter.12.cloned.1.call-done = f32[96,6144]{1,0:T(8,128)} async-done(((f32[768,6144]{1,0:T(8,128)}), f32[96,6144]{1,0:T(8,128)}) %reduce-scatter.12.cloned.1.call-update) | async-done | bytes 2359312 | tf_op jit(solution)/shard_map/reduce_scatter | solution.py:240
  1416.2 11.8 all-gather.16.cloned.1.call-done
  1430.6 50.4 %all-reduce.5.cloned.1.call-done = (bf16[96,768]{1,0:T(8,128)(2,1)}, bf16[96,6144]{1,0:T(8,128)(2,1)}, bf16[384,768]{1,0:T(8,128)(2,1)}) async-done(((bf16[96,768]{1,0:T(8,128)(2,1)}, bf16[96,6144]{1,0:T(8,128)(2,1)}, bf16[384,768]{1,0:T(8,128)(2,1)}), (bf16[96,768]{1,0:T(8,128)(2,1)}, bf16[96,6144]{1,0:T(8,128)(2,1)}, bf16[384,768]{1,0:T(8,128)(2,1)})) %all-reduce.5.cloned.1.call-update) | async-done | bytes 1916944 | tf_op jit(solution)/shard_map/psum | solution.py:246
  1493.5 21.8 %psum.39 = f32[]{:T(128)} all-reduce(f32[]{:T(128)S(6)} %add.229), channel_id=1, replica_groups=mesh['dp'=8,'head'=4] {'dp'}, use_global_device_ids=true, to_apply=%region_36.37 | all-reduce | flops 1 | bytes 8 | tf_op jit(solution)/shard_map/psum | solution.py:254
  (296 shorter events, 298.0 us)
Async XLA Ops:
  7.2 71.5 %all-gather.8.cloned.1.call-start = ((), (), s32[]{:S(2)}) async-start(), calls=%async_computation.9 | async-start | bytes 3981312 | tf_op jit(solution)/shard_map/all_gather | solution.py:102
  92.4 44.9 %all-to-all-start = ((bf16[768,3,4,192]{0,3,1,2:T(8,128)(2,1)}), bf16[768,3,4,192]{0,3,1,2:T(8,128)(2,1)S(1)}, u32[]{:S(2)}, u32[]{:S(2)}) async-start(bf16[768,3,4,192]{0,3,1,2:T(8,128)(2,1)} %copy.108), calls=%async_computation | async-start | bytes 7077888 | tf_op jit(solution)/shard_map/all_to_all | solution.py:115
  96.1 201.3 %all-gather.10.cloned.1.call-start = ((), (), s32[]{:S(2)}) async-start(), calls=%async_computation.10 | async-start | bytes 1327104 | tf_op jit(solution)/shard_map/all_gather | solution.py:103
  97.8 205.1 %all-gather.12.cloned.1.call-start = ((), (), s32[]{:S(2)}) async-start(), calls=%async_computation.11 | async-start | bytes 10616832 | tf_op jit(solution)/shard_map/all_gather | solution.py:104
  201.6 12.5 copy-start.36
  238.5 41.1 %all-to-all-start.1 = ((bf16[4,2,73728]{2,1,0:T(2,128)(2,1)}), bf16[4,2,73728]{2,1,0:T(2,128)(2,1)}, u32[]{:S(2)}, u32[]{:S(2)}) async-start(bf16[4,2,73728]{2,1,0:T(2,128)(2,1)} %reshape.391), calls=%async_computation.1 | async-start | bytes 2359296 | tf_op jit(solution)/shard_map/all_to_all | solution.py:145
  242.8 117.7 %all-gather.14.cloned.1.call-start = ((), (), s32[]{:S(2)}) async-start(), calls=%async_computation.12 | async-start | bytes 5308416 | tf_op jit(solution)/shard_map/all_gather | solution.py:105
  279.5 80.9 %copy-start.33 = (f32[768]{0:T(1024)}, f32[768]{0:T(1024)S(1)}, u32[]{:S(2)}) copy-start(f32[768]{0:T(1024)S(1)} %get-tuple-element.236) | copy-start | bytes 9220
  279.5 135.0 %copy-start.31 = (f32[768]{0:T(1024)}, f32[768]{0:T(1024)S(1)}, u32[]{:S(2)}) copy-start(f32[768]{0:T(1024)S(1)} %get-tuple-element.237) | copy-start | bytes 9220
  300.7 113.9 %copy-start.25 = (f32[768]{0:T(1024)}, f32[768]{0:T(1024)S(1)}, u32[]{:S(2)}) copy-start(f32[768]{0:T(1024)S(1)} %broadcast_multiply_fusion.1) | copy-start | bytes 9220
  303.0 111.6 %copy-start.29 = (f32[768]{0:T(1024)}, f32[768]{0:T(1024)S(1)}, u32[]{:S(2)}) copy-start(f32[768]{0:T(1024)S(1)} %fusion.58) | copy-start | bytes 9220
  314.6 6.8 copy-start
  375.1 19.0 %copy-start.46 = (f32[768]{0:T(1024)}, f32[768]{0:T(1024)S(1)}, u32[]{:S(2)}) copy-start(f32[768]{0:T(1024)S(1)} %negate_multiply_fusion.2) | copy-start | bytes 9220
  394.1 19.8 %copy-start.41 = (f32[768]{0:T(1024)S(1)}, f32[768]{0:T(1024)}, u32[]{:S(2)}) copy-start(f32[768]{0:T(1024)} %copy-done.40) | copy-start | bytes 9220
  419.9 20.2 %all-to-all-start.2 = ((bf16[768,4,192]{0,2,1:T(8,128)(2,1)}), bf16[768,4,192]{0,2,1:T(8,128)(2,1)}, u32[]{:S(2)}, u32[]{:S(2)}) async-start(bf16[768,4,192]{0,2,1:T(8,128)(2,1)} %bitcast.169), calls=%async_computation.2 | async-start | bytes 2359296 | tf_op jit(solution)/shard_map/all_to_all | solution.py:178
  424.2 361.5 %reduce-scatter.16.cloned.1.call-start = ((), (), s32[]{:S(2)}) async-start(), calls=%async_computation.17 | async-start | bytes 7962624 | tf_op jit(solution)/shard_map/reduce_scatter | solution.py:238
  443.3 7.4 copy-start.38
  659.3 190.9 %reduce-scatter.18.cloned.1.call-start = ((), (), s32[]{:S(2)}) async-start(), calls=%async_computation.18 | async-start | bytes 442368
  665.8 257.0 %reduce-scatter.10.cloned.1.call-start = ((), (), s32[]{:S(2)}) async-start(), calls=%async_computation.13 | async-start | bytes 2654208 | tf_op jit(solution)/shard_map/reduce_scatter | solution.py:239
  668.4 420.7 %reduce-scatter.14.cloned.1.call-start = ((), (), s32[]{:S(2)}) async-start(), calls=%async_computation.15 | async-start | bytes 10616832 | tf_op jit(solution)/shard_map/reduce_scatter | solution.py:241
  678.9 727.1 %reduce-scatter.12.cloned.1.call-start = ((), (), s32[]{:S(2)}) async-start(), calls=%async_computation.14 | async-start | bytes 21233664 | tf_op jit(solution)/shard_map/reduce_scatter | solution.py:240
  701.2 87.2 %copy-start.14 = (bf16[768,768]{0,1:T(8,128)(2,1)S(1)}, bf16[768,768]{0,1:T(8,128)(2,1)}, u32[]{:S(2)}) copy-start(bf16[768,768]{0,1:T(8,128)(2,1)} %get-tuple-element.300) | copy-start | bytes 3538948
  701.2 726.8 %all-gather.16.cloned.1.call-start = ((), (), s32[]{:S(2)}) async-start(), calls=%async_computation.16 | async-start | bytes 2211840 | tf_op jit(solution)/shard_map/all_gather | solution.py:245
  787.7 693.2 %all-reduce.5.cloned.1.call-start = ((), (), s32[]{:S(2)}) async-start(), calls=%async_computation.19 | async-start | bytes 3833856 | tf_op jit(solution)/shard_map/psum | solution.py:246
  1091.3 317.5 %copy-start.9 = (f32[768,768]{0,1:T(8,128)S(1)}, f32[768,768]{0,1:T(8,128)}, u32[]{:S(2)}) copy-start(f32[768,768]{0,1:T(8,128)} %copy-done.7) | copy-start | bytes 7077892
  1490.2 25.8 %copy-start.16 = (f32[96,2304]{1,0:T(8,128)S(1)}, f32[96,2304]{1,0:T(8,128)}, u32[]{:S(2)}) copy-start(f32[96,2304]{1,0:T(8,128)} %param.28) | copy-start | bytes 2654212
  1490.2 25.8 %copy-start.27 = (f32[96,2304]{1,0:T(8,128)S(1)}, f32[96,2304]{1,0:T(8,128)}, u32[]{:S(2)}) copy-start(f32[96,2304]{1,0:T(8,128)} %param.33) | copy-start | bytes 2654212
  1490.2 25.8 %copy-start.28 = (f32[96,2304]{1,0:T(8,128)S(1)}, f32[96,2304]{1,0:T(8,128)}, u32[]{:S(2)}) copy-start(f32[96,2304]{1,0:T(8,128)} %param.38) | copy-start | bytes 2654212
  1490.2 28.0 %copy-start.20 = (f32[96,768]{1,0:T(8,128)S(1)}, f32[96,768]{1,0:T(8,128)}, u32[]{:S(2)}) copy-start(f32[96,768]{1,0:T(8,128)} %param.29) | copy-start | bytes 884740
  1490.3 28.0 %copy-start.35 = (bf16[96,768]{1,0:T(8,128)(2,1)S(1)}, bf16[96,768]{1,0:T(8,128)(2,1)}, u32[]{:S(2)}) copy-start(bf16[96,768]{1,0:T(8,128)(2,1)} %get-tuple-element.265) | copy-start | bytes 442372
  1516.1 5.1 copy-start.6
  1516.1 5.1 copy-start.17
  (44 other events, 105.3 us)
Sparse Core Ops, SparseCore 0:
  10.8 67.8 all-gather.7
  99.7 40.1 all-gather.9
  142.7 136.8 all-gather.11
  282.1 78.2 all-gather.13
  659.4 126.2 reduce-scatter.15
  789.7 60.4 reduce-scatter.17
  854.7 68.0 reduce-scatter.9
  926.8 162.3 reduce-scatter.13
  1093.6 312.3 reduce-scatter.11
  1408.0 19.8 all-gather.15
  1431.9 49.0 all-reduce.4
